TPU v7x, 128 devices: a whole 4x4x4 slice. The times are simulated.
128 devices in a mesh: sec: 16 (over y, z_lo, core), head: 8 (over z_hi, x).
Axes of the slice: x: 4, y: 4, z: 4 (z_hi: 2, z_lo: 2; z = z_hi * 2 + z_lo), core: 2. Of those that a mesh axis runs over, the one named last changes fastest.
Arguments:
- tokens: bfloat16 [16384, 4096], P('sec')
- w_query: bfloat16 [4096, 4096], P(None, 'head')
- w_key: bfloat16 [4096, 1024], P(None, 'head')
- w_value: bfloat16 [4096, 1024], P(None, 'head'), may hold values from -0.09375 to 0.09375
- w_out: bfloat16 [4096, 4096], P('head'), may hold values from -0.375 to 0.375
- key_start: int32 [64], replicated, may hold values from 0 to 16128, as said below
Outputs:
- mixed: bfloat16 [16384, 4096], P('sec', 'head')
Inputs may be any that keep to these rules, and one draw needn't show every extreme that they name: key_start[c] is a multiple of 256 and at most c * 256; the last block's entry is (64 - 1) * 256.
All inputs are finite; a program needn't handle non-finite values.
Results may differ from a plain program's by a relative error of at most 0.015.
The roundings to bfloat16 on the way count: a program that leaves them out, or rounds other values in their place, can miss the bound.
Values may be sent and summed in bfloat16 or wider, within the bound.
A program may use at most 128 MiB of HBM per device.

v0:
```python
import math
import jax
import jax.numpy as jnp
from jax import lax
from jax.sharding import PartitionSpec as P

QH = 32
KVH = 8
HD = 128
SPAN = 256


def rotate(heads_data, position):
    midway = heads_data.shape[-1] // 2
    frequency = jnp.float32(500000.0) ** (
        -(jnp.arange(midway, dtype=jnp.float32) * 2.0) / heads_data.shape[-1]
    )
    angle = position.astype(jnp.float32)[:, None] * frequency[None, :]
    cosine = jnp.cos(angle)[:, None, :]
    sine = jnp.sin(angle)[:, None, :]
    first_half = heads_data[..., :midway]
    second_half = heads_data[..., midway:]
    return jnp.concatenate(
        [first_half * cosine - second_half * sine, second_half * cosine + first_half * sine],
        axis=-1,
    )


def attend(query_sets, key_start, keys, values, local_groups, groups):
    table = jnp.arange(key_start.shape[0], dtype=jnp.int32)
    scale = HD ** (-0.5)
    prepared = []
    for queries, query_position in query_sets:
        number = queries.shape[0]
        span_index = query_position // SPAN
        lower = jnp.sum(
            jnp.where(span_index[:, None] == table[None, :], key_start[None, :], 0), axis=1
        )
        shaped = queries.reshape(number, local_groups, groups, HD)
        prepared.append((shaped, query_position, lower, jnp.min(lower), jnp.max(query_position)))
    shaped, query_position, lower, first_visible, last_query = prepared[0]
    number = shaped.shape[0]
    initial = [
        (
            jnp.full((local_groups, groups, number), -1e30, jnp.float32),
            jnp.zeros((local_groups, groups, number), jnp.float32),
            jnp.zeros((local_groups, groups, number, HD), jnp.float32),
        )
    ]
    key_piece = lax.all_gather(keys, "sec", axis=0, tiled=True)
    value_piece = lax.all_gather(values, "sec", axis=0, tiled=True)
    length = key_piece.shape[0]
    width = math.gcd(length, 1024)
    key_view = key_piece.reshape(length, local_groups, HD)
    value_view = value_piece.reshape(length, local_groups, HD)
    shaped, query_position, lower, first_visible, last_query = prepared[0]

    def one_block(
        index,
        state,
        shaped=shaped,
        query_position=query_position,
        lower=lower,
        first_visible=first_visible,
        last_query=last_query,
    ):
        offset = index * width

        def update(current):
            largest, weight_sum, gathered = current
            key_block = lax.dynamic_slice_in_dim(key_view, offset, width, 0)
            value_block = lax.dynamic_slice_in_dim(value_view, offset, width, 0)
            key_position = offset + jnp.arange(width, dtype=jnp.int32)
            scores = (
                jnp.einsum("qhgd,jhd->hgqj", shaped, key_block, preferred_element_type=jnp.float32)
                * scale
            )
            allowed = (key_position[None, :] >= lower[:, None]) & (
                key_position[None, :] <= query_position[:, None]
            )
            scores = jnp.where(allowed[None, None], scores, -jnp.inf)
            newest = jnp.maximum(largest, jnp.max(scores, axis=-1))
            weights = jnp.exp(scores - newest[..., None])
            factor = jnp.exp(largest - newest)
            weight_sum = weight_sum * factor + jnp.sum(weights, axis=-1)
            gathered = gathered * factor[..., None] + jnp.einsum(
                "hgqj,jhd->hgqd",
                weights.astype(jnp.bfloat16),
                value_block,
                preferred_element_type=jnp.float32,
            )
            return (newest, weight_sum, gathered)

        def keep_state(current):
            return current

        needed = (offset <= last_query) & (offset + width > first_visible)
        return lax.cond(needed, update, keep_state, state)

    updated = [lax.fori_loop(0, length // width, one_block, tuple(initial)[0])]
    states = tuple(updated)
    results = []
    for largest, weight_sum, gathered in states:
        number = gathered.shape[2]
        result = gathered / weight_sum[..., None]
        results.append(
            result.transpose(2, 0, 1, 3)
            .reshape(number, local_groups * groups * HD)
            .astype(jnp.bfloat16)
        )
    return results


def shards(tokens, w_query, w_key, w_value, w_out, key_start):
    rows = tokens.shape[0]
    local_groups = w_key.shape[1] // HD
    groups = QH // KVH
    section = lax.axis_index("sec")
    position = section * rows + jnp.arange(rows, dtype=jnp.int32)
    query = rotate(
        jnp.dot(tokens, w_query, preferred_element_type=jnp.float32).reshape(
            rows, local_groups * groups, HD
        ),
        position,
    )
    query = query.astype(jnp.bfloat16).reshape(rows, local_groups * groups * HD)
    keys = rotate(
        jnp.dot(tokens, w_key, preferred_element_type=jnp.float32).reshape(rows, local_groups, HD),
        position,
    )
    keys = keys.astype(jnp.bfloat16).reshape(rows, local_groups * HD)
    values = jnp.dot(tokens, w_value, preferred_element_type=jnp.float32).astype(jnp.bfloat16)
    attended = attend([(query, position)], key_start, keys, values, local_groups, groups)[0]
    terms = jnp.dot(attended, w_out, preferred_element_type=jnp.float32)
    mixed = lax.psum_scatter(terms.astype(jnp.bfloat16), "head", scatter_dimension=1, tiled=True)
    return mixed


def solution(mesh):
    placed = (
        P("sec", None),
        P(None, "head"),
        P(None, "head"),
        P(None, "head"),
        P("head", None),
        P(),
    )
    return jax.shard_map(
        shards, mesh=mesh, in_specs=placed, out_specs=P("sec", "head"), check_vma=False
    )
```

profile of v0, /device:TPU:0, one launch (start us, length us, event | category | flops | bytes accessed | tf_op | source)
XLA Modules:
  0.0 434.9 jit_solution(15608981831324070247)
XLA Ops:
  6.6 1.2 copy-done
  7.8 6.4 %convolution_bitcast_fusion = f32[1024,1,128]{0,2,1:T(8,128)S(1)} fusion(bf16[1024,4096]{1,0:T(8,128)(2,1)} %param.10, bf16[4096,128]{1,0:T(8,128)(2,1)S(1)} %copy-done), kind=kOutput, calls=%fused_computation.31 | convolution fusion | flops 1073741824 | bytes 9961472 | tf_op jit(solution)/shard_map/dot_general | solution.py:128
  14.1 1.2 fusion.33
  15.3 0.7 pad_maximum_fusion.1
  16.0 0.0 all-gather.3.cloned.1.call-update
  16.0 0.0 all-gather.5.cloned.1.call-start
  16.1 6.4 %convolution_convert_fusion.1 = bf16[1024,128]{1,0:T(8,128)(2,1)} fusion(bf16[1024,4096]{1,0:T(8,128)(2,1)} %param.10, bf16[4096,128]{1,0:T(8,128)(2,1)S(1)} %copy-done.3), kind=kOutput, calls=%fused_computation.32 | convolution fusion | flops 1073872896 | bytes 9699328 | tf_op jit(solution)/shard_map/dot_general | solution.py:132
  22.5 0.0 reduce-scatter.2.cloned.1.call-start
  22.6 8.3 %fusion.40 = f32[1024,512]{0,1:T(8,128)S(1)} fusion(bf16[1024,4096]{1,0:T(8,128)(2,1)} %param.10, bf16[4096,512]{1,0:T(8,128)(2,1)} %param.11), kind=kOutput, calls=%fused_computation.66 | convolution fusion | flops 4294967296 | bytes 14680064 | tf_op jit(solution)/shard_map/dot_general | solution.py:121
  30.8 1.2 fusion.39
  32.1 1.8 copy.23
  33.9 1.9 copy.22
  35.9 0.6 add_select_fusion
  36.5 0.1 select_reduce_fusion
  36.6 0.7 reduce_min.9
  37.3 1.9 multiply_cosine_fusion
  39.2 2.2 fusion.22
  41.3 0.6 pad_maximum_fusion
  41.9 14.0 %all-gather.3.cloned.1.call-done = bf16[16384,128]{0,1:T(8,128)(2,1)} async-done(((bf16[1024,128]{0,1:T(8,128)(2,1)}), bf16[16384,128]{0,1:T(8,128)(2,1)}) %all-gather.3.cloned.1.call-update) | async-done | bytes 4194320 | tf_op jit(solution)/shard_map/all_gather | solution.py:50
  55.9 6.4 %copy.19 = bf16[16384,1,128]{2,0,1:T(8,128)(2,1)} copy(bf16[16384,1,128]{0,2,1:T(8,128)(2,1)} %bitcast.72) | data formatting | bytes 8388608
  62.3 32.7 %all-gather.5.cloned.1.call-done = bf16[16384,128]{1,0:T(8,128)(2,1)} async-done(((bf16[1024,128]{1,0:T(8,128)(2,1)}), bf16[16384,128]{1,0:T(8,128)(2,1)}) %all-gather.5.cloned.1.call-update) | async-done | bytes 4194320 | tf_op jit(solution)/shard_map/all_gather | solution.py:51
  95.0 0.1 broadcast_in_dim.28
  95.2 35.4 %while.18 = (s32[]{:T(128)}, f32[1,4,1024]{2,1,0:T(4,128)S(1)}, f32[1,4,1024]{2,1,0:T(4,128)S(1)}, f32[1,4,1024,128]{3,2,1,0:T(8,128)S(1)}, s32[]{:T(128)}, /*in...) while((s32[]{:T(128)}, f32[1,4,1024]{2,1,0:T(4,128)S(1)}, ...), condition=%wide.region_8.9_spmd.clone, body=%wide.region_3.8_spmd.clone.sunk | while | flops 2197829632 | bytes 60584296 | solution.py:100
  96.7 14.2 %conditional.3 = ((f32[1,4,1024]{2,1,0:T(4,128)S(1)}, f32[1,4,1024]{2,1,0:T(4,128)S(1)}, f32[1,4,1024,128]{3,2,1,0:T(8,128)S(1)})) conditional(s32[]{:T(128)} %convert_element_type.63, (f32[1,4,1024]{2,1,0:T(4,128)S(1)}, f32[1,4,1024]{2,1,0:T(4,128)S(1)}, f32[1,4,1024,128]{3,2,1,0:T(8,128)S(1)}) %tuple.53, (s32[]{:T(128)}, s32[1024]{0:T(1024)S(1)}, ...), branch_computations={%region_4.4_spmd, %region_5.7_spmd} | conditional | flops 2197829632 | bytes 60579924 | solution.py:98
  96.7 0.9 compare_and_fusion
  97.6 3.8 fusion.4
  101.4 5.8 %bitcast_add_fusion = f32[1,4,1024,128]{3,2,1,0:T(8,128)S(1)} fusion(f32[1,4,1024,128]{3,2,1,0:T(8,128)S(1)} %get-tuple-element.213, f32[1024,1024,4]{1,0,2:T(8,128)S(1)} %get-tuple-element.323, f32[4,1024]{1,0:T(4,128)S(1)} %bitcast.70, pred[1024,1024]{0,1:T(8,128)(4,1)S(1)} %compare_and_fusion, f32[4,1024]{1,0:T(4,128)S(1)} %get-tuple-element.320, ...), kind=kOutput, calls=%fused_computation.10 | convolution fusion | flops 1091567616 | bytes 22315012 | tf_op jit(solution)/shard_map/while/body/eval_jaxpr/cond/branch_1_fun/hgqj,jhd->hgqd/dot_general | solution.py:86
  107.2 3.7 fusion.3
  130.6 1.9 copy.20
  132.4 1.8 divide_convert_fusion
  134.3 9.0 %convolution_convert_fusion = bf16[1024,4096]{1,0:T(8,128)(2,1)} fusion(bf16[1024,512]{0,1:T(8,128)(2,1)S(1)} %bitcast.74, bf16[512,4096]{1,0:T(8,128)(2,1)} %param.14), kind=kOutput, calls=%fused_computation.27 | convolution fusion | flops 4299161600 | bytes 13631488 | tf_op jit(solution)/shard_map/dot_general | solution.py:134
  143.3 285.1 %reduce-scatter.2.cloned.1.call-done = bf16[1024,512]{1,0:T(8,128)(2,1)} async-done(((bf16[1024,4096]{1,0:T(8,128)(2,1)}), bf16[1024,512]{1,0:T(8,128)(2,1)}) %reduce-scatter.2.cloned.1.call-update) | async-done | bytes 1048592 | tf_op jit(solution)/shard_map/reduce_scatter | solution.py:135
  (49 shorter events, 0.4 us)
Async XLA Ops:
  6.5 1.2 copy-start
  6.5 49.4 %all-gather.3.cloned.1.call-start = ((), (), s32[]{:S(2)}) async-start(), calls=%async_computation.1 | async-start | bytes 4456448 | tf_op jit(solution)/shard_map/all_gather | solution.py:50
  7.8 8.3 %copy-start.3 = (bf16[4096,128]{1,0:T(8,128)(2,1)S(1)}, bf16[4096,128]{1,0:T(8,128)(2,1)}, u32[]{:S(2)}) copy-start(bf16[4096,128]{1,0:T(8,128)(2,1)} %param.13) | copy-start | bytes 3145732
  16.0 79.0 %all-gather.5.cloned.1.call-start = ((), (), s32[]{:S(2)}) async-start(), calls=%async_computation.2 | async-start | bytes 4456448 | tf_op jit(solution)/shard_map/all_gather | solution.py:51
  22.5 405.8 %reduce-scatter.2.cloned.1.call-start = ((), (), s32[]{:S(2)}) async-start(), calls=%async_computation.3 | async-start | bytes 9437184 | tf_op jit(solution)/shard_map/reduce_scatter | solution.py:135
  32.1 4.4 %copy-start.2 = (s32[64]{0:T(128)S(1)}, s32[64]{0:T(128)}, u32[]{:S(2)}) copy-start(s32[64]{0:T(128)} %param.15) | copy-start | bytes 772
  143.3 285.1 %copy-start.1 = (bf16[4096,128]{1,0:T(8,128)(2,1)S(1)}, bf16[4096,128]{1,0:T(8,128)(2,1)}, u32[]{:S(2)}) copy-start(bf16[4096,128]{1,0:T(8,128)(2,1)} %param.12) | copy-start | bytes 3145732
Sparse Core Ops, SparseCore 0:
  16.2 39.6 all-gather.2
  57.6 37.3 all-gather.4
  143.4 284.9 reduce-scatter.1
where the time goes:
time: 436 us; the launch traced here: 435 us
  waiting for transfers between devices  332 us (76%)
  matrix products  39.6 us (9%)
  loops' own time  21.2 us (5%)
  local copies, waits for them, and re-layouts  14.7 us (3%)
  other arithmetic  14.3 us (3%)
  between operations  13.2 us (3%)
    reduce_scatter x1, waiting for transfers between devices, shards(): lax.psum_scatter(terms.astype(jnp.bfloat16), 'head', scatter_dimension=1,...  285 us
    all_gather x1, waiting for transfers between devices, attend(): value_piece = lax.all_gather(values, 'sec', axis=0, tiled=True)  32.7 us
    another operation x1, loops' own time, attend(): updated = [lax.fori_loop(0, length // width, one_block, tuple(initial)[0])]  20.9 us
    all_gather x1, waiting for transfers between devices, attend(): key_piece = lax.all_gather(keys, 'sec', axis=0, tiled=True)  14 us
    unnamed x11, local copies, waits for them, and re-layouts  11.4 us
    dot_general x1, matrix products, shards(): terms = jnp.dot(attended, w_out, preferred_element_type=jnp.float32)  8.97 us
  transfers between devices with their start and end apart: 3, of which 3 were waited for; matrix products, arithmetic and copies ran while one was open for 7% of the time, Pallas kernels for 0%

commit v1 on v0

--- a/solution.py
+++ b/solution.py
@@ -48,7 +48,9 @@
         )
     ]
     key_piece = lax.all_gather(keys, "sec", axis=0, tiled=True)
-    value_piece = lax.all_gather(values, "sec", axis=0, tiled=True)
+    value_piece = jnp.concatenate(
+        lax.all_to_all(jnp.stack([values] * lax.axis_size("sec")), "sec", 0, 0), axis=0
+    )
     length = key_piece.shape[0]
     width = math.gcd(length, 1024)
     key_view = key_piece.reshape(length, local_groups, HD)

time: 436 us -> 451 us (1.034)
  starting transfers between devices: 0.09 us -> 6.31 us
    all_gather x1 -> x0, waiting for transfers between devices: 32.7 us -> none  [attend(): value_piece = lax.all_gather(values, 'sec', axis=0, tiled=True)]
    all_gather x1, waiting for transfers between devices: 14 us -> 46.3 us  [attend(): key_piece = lax.all_gather(keys, 'sec', axis=0, tiled=True)]
    all_to_all x0 -> x1, starting transfers between devices: none -> 6.09 us  [attend(): lax.all_to_all(jnp.stack([values] * lax.axis_size('sec')), 'sec', 0, 0)]
    reduce_scatter x1, waiting for transfers between devices: 285 us -> 290 us  [shards(): lax.psum_scatter(terms.astype(jnp.bfloat16), 'head', scatter_dimension=1,...]
  transfers between devices with their start and end apart: 3 -> 3, of which waited for: 3 -> 2; matrix products, arithmetic and copies ran while one was open for 7% -> 8% of each run, Pallas kernels for 0% -> 0%
where the time goes in v1:
time: 451 us; the launch traced here: 449 us
  waiting for transfers between devices  336 us (75%)
  matrix products  39 us (9%)
  loops' own time  22.5 us (5%)
  local copies, waits for them, and re-layouts  17.4 us (4%)
  other arithmetic  14.3 us (3%)
  between operations  13.5 us (3%)
  starting transfers between devices  6.31 us (1%)
    reduce_scatter x1, waiting for transfers between devices, shards(): lax.psum_scatter(terms.astype(jnp.bfloat16), 'head', scatter_dimension=1,...  290 us
    all_gather x1, waiting for transfers between devices, attend(): key_piece = lax.all_gather(keys, 'sec', axis=0, tiled=True)  46.3 us
    another operation x1, loops' own time, attend(): updated = [lax.fori_loop(0, length // width, one_block, tuple(initial)[0])]  22.2 us
    unnamed x11, local copies, waits for them, and re-layouts  11.4 us
  transfers between devices with their start and end apart: 3, of which 2 were waited for; matrix products, arithmetic and copies ran while one was open for 8% of the time, Pallas kernels for 0%

profile of v1, /device:TPU:0, one launch (start us, length us, event | category | flops | bytes accessed | tf_op | source)
XLA Modules:
  0.0 449.2 jit_solution(6983356513757046712)
XLA Ops:
  6.6 1.2 copy-done
  7.8 6.4 %convolution_bitcast_fusion = f32[1024,1,128]{0,2,1:T(8,128)S(1)} fusion(bf16[1024,4096]{1,0:T(8,128)(2,1)} %param.10, bf16[4096,128]{1,0:T(8,128)(2,1)S(1)} %copy-done), kind=kOutput, calls=%fused_computation.31 | convolution fusion | flops 1073741824 | bytes 9961472 | tf_op jit(solution)/shard_map/dot_general | solution.py:130
  14.1 1.2 fusion.33
  15.3 0.7 pad_maximum_fusion.1
  16.0 0.0 all-gather.2.cloned.1.call-update
  16.0 5.7 %convolution_convert_fusion.1 = bf16[1024,128]{1,0:T(8,128)(2,1)S(1)} fusion(bf16[1024,4096]{1,0:T(8,128)(2,1)} %param.10, bf16[4096,128]{1,0:T(8,128)(2,1)S(1)} %copy-done.3), kind=kOutput, calls=%fused_computation.32 | convolution fusion | flops 1073872896 | bytes 9699328 | tf_op jit(solution)/shard_map/dot_general | solution.py:134
  21.8 2.8 stack.2
  24.5 6.1 %all-to-all-start = ((bf16[16,1024,128]{2,1,0:T(8,128)(2,1)}), bf16[16,1024,128]{2,1,0:T(8,128)(2,1)}, u32[]{:S(2)}, u32[]{:S(2)}) async-start(bf16[16,1024,128]{2,1,0:T(8,128)(2,1)} %stack.2), calls=%async_computation | async-start | bytes 8388608 | tf_op jit(solution)/shard_map/all_to_all | solution.py:52
  30.6 0.2 reduce-scatter.2.cloned.1.call-start
  30.8 8.4 %fusion.40 = f32[1024,512]{0,1:T(8,128)S(1)} fusion(bf16[1024,4096]{1,0:T(8,128)(2,1)} %param.10, bf16[4096,512]{1,0:T(8,128)(2,1)} %param.11), kind=kOutput, calls=%fused_computation.66 | convolution fusion | flops 4294967296 | bytes 14680064 | tf_op jit(solution)/shard_map/dot_general | solution.py:123
  39.3 1.2 fusion.39
  40.5 1.8 copy.23
  42.3 1.9 copy.22
  44.3 0.6 add_select_fusion
  44.9 0.1 select_reduce_fusion
  45.0 0.7 reduce_min.9
  45.7 1.9 multiply_cosine_fusion
  47.6 2.1 fusion.22
  49.7 0.6 pad_maximum_fusion
  50.3 46.3 %all-gather.2.cloned.1.call-done = bf16[16384,128]{0,1:T(8,128)(2,1)} async-done(((bf16[1024,128]{0,1:T(8,128)(2,1)}), bf16[16384,128]{0,1:T(8,128)(2,1)}) %all-gather.2.cloned.1.call-update) | async-done | bytes 4194320 | tf_op jit(solution)/shard_map/all_gather | solution.py:50
  96.6 6.4 %copy.19 = bf16[16384,1,128]{2,0,1:T(8,128)(2,1)} copy(bf16[16384,1,128]{0,2,1:T(8,128)(2,1)} %bitcast.72) | data formatting | bytes 8388608
  103.1 0.1 broadcast_in_dim.28
  103.2 36.7 %while.18 = (s32[]{:T(128)}, f32[1,4,1024]{2,1,0:T(4,128)S(1)}, f32[1,4,1024]{2,1,0:T(4,128)S(1)}, f32[1,4,1024,128]{3,2,1,0:T(8,128)S(1)}, s32[]{:T(128)}, /*in...) while((s32[]{:T(128)}, f32[1,4,1024]{2,1,0:T(4,128)S(1)}, ...), condition=%wide.region_8.9_spmd.clone, body=%wide.region_3.8_spmd.clone.sunk | while | flops 2197829632 | bytes 60584296 | solution.py:102
  104.8 14.2 %conditional.3 = ((f32[1,4,1024]{2,1,0:T(4,128)S(1)}, f32[1,4,1024]{2,1,0:T(4,128)S(1)}, f32[1,4,1024,128]{3,2,1,0:T(8,128)S(1)})) conditional(s32[]{:T(128)} %convert_element_type.63, (f32[1,4,1024]{2,1,0:T(4,128)S(1)}, f32[1,4,1024]{2,1,0:T(4,128)S(1)}, f32[1,4,1024,128]{3,2,1,0:T(8,128)S(1)}) %tuple.53, (s32[]{:T(128)}, s32[1024]{0:T(1024)S(1)}, ...), branch_computations={%region_4.4_spmd, %region_5.7_spmd} | conditional | flops 2197829632 | bytes 60579924 | solution.py:100
  104.8 0.9 compare_and_fusion
  105.7 3.8 fusion.4
  109.6 5.8 %bitcast_add_fusion = f32[1,4,1024,128]{3,2,1,0:T(8,128)S(1)} fusion(f32[1,4,1024,128]{3,2,1,0:T(8,128)S(1)} %get-tuple-element.213, f32[1024,1024,4]{1,0,2:T(8,128)S(1)} %get-tuple-element.323, f32[4,1024]{1,0:T(4,128)S(1)} %bitcast.70, pred[1024,1024]{0,1:T(8,128)(4,1)S(1)} %compare_and_fusion, f32[4,1024]{1,0:T(4,128)S(1)} %get-tuple-element.320, ...), kind=kOutput, calls=%fused_computation.10 | convolution fusion | flops 1091567616 | bytes 22315012 | tf_op jit(solution)/shard_map/while/body/eval_jaxpr/cond/branch_1_fun/hgqj,jhd->hgqd/dot_general | solution.py:88
  115.3 3.7 fusion.3
  139.9 1.9 copy.20
  141.8 1.8 divide_convert_fusion
  143.7 9.0 %convolution_convert_fusion = bf16[1024,4096]{1,0:T(8,128)(2,1)} fusion(bf16[1024,512]{0,1:T(8,128)(2,1)S(1)} %bitcast.74, bf16[512,4096]{1,0:T(8,128)(2,1)} %param.14), kind=kOutput, calls=%fused_computation.27 | convolution fusion | flops 4299161600 | bytes 13631488 | tf_op jit(solution)/shard_map/dot_general | solution.py:136
  152.7 289.7 %reduce-scatter.2.cloned.1.call-done = bf16[1024,512]{1,0:T(8,128)(2,1)} async-done(((bf16[1024,4096]{1,0:T(8,128)(2,1)}), bf16[1024,512]{1,0:T(8,128)(2,1)}) %reduce-scatter.2.cloned.1.call-update) | async-done | bytes 1048592 | tf_op jit(solution)/shard_map/reduce_scatter | solution.py:137
  (49 shorter events, 0.4 us)
Async XLA Ops:
  6.5 1.2 copy-start
  6.5 90.1 %all-gather.2.cloned.1.call-start = ((), (), s32[]{:S(2)}) async-start(), calls=%async_computation.2 | async-start | bytes 4456448 | tf_op jit(solution)/shard_map/all_gather | solution.py:50
  7.8 8.3 %copy-start.3 = (bf16[4096,128]{1,0:T(8,128)(2,1)S(1)}, bf16[4096,128]{1,0:T(8,128)(2,1)}, u32[]{:S(2)}) copy-start(bf16[4096,128]{1,0:T(8,128)(2,1)} %param.13) | copy-start | bytes 3145732
  24.5 78.5 %all-to-all-start = ((bf16[16,1024,128]{2,1,0:T(8,128)(2,1)}), bf16[16,1024,128]{2,1,0:T(8,128)(2,1)}, u32[]{:S(2)}, u32[]{:S(2)}) async-start(bf16[16,1024,128]{2,1,0:T(8,128)(2,1)} %stack.2), calls=%async_computation | async-start | bytes 8388608 | tf_op jit(solution)/shard_map/all_to_all | solution.py:52
  30.6 411.8 %reduce-scatter.2.cloned.1.call-start = ((), (), s32[]{:S(2)}) async-start(), calls=%async_computation.3 | async-start | bytes 9437184 | tf_op jit(solution)/shard_map/reduce_scatter | solution.py:137
  40.5 4.4 copy-start.2
  152.6 289.7 %copy-start.1 = (bf16[4096,128]{1,0:T(8,128)(2,1)S(1)}, bf16[4096,128]{1,0:T(8,128)(2,1)}, u32[]{:S(2)}) copy-start(bf16[4096,128]{1,0:T(8,128)(2,1)} %param.12) | copy-start | bytes 3145732
Sparse Core Ops, SparseCore 0:
  16.2 80.4 all-gather.1
  152.8 289.5 reduce-scatter.1
